TPU v7x, 256 devices: a whole 4x4x8 slice. The times are simulated.
256 devices in a mesh: row: 8 (over z_hi, core), col: 32 (over x, z_lo, y).
Axes of the slice: x: 4, y: 4, z: 8 (z_hi: 4, z_lo: 2; z = z_hi * 2 + z_lo), core: 2. Of those that a mesh axis runs over, the one named last changes fastest.
Arguments:
- features: bfloat16 [131072, 128], P(('row', 'col')), may hold values from -6 to 6
- weight: bfloat16 [128, 128], replicated, may hold values from -0.5 to 0.5
- bias: float32 [128], replicated, may hold values from -3 to 3
- cotangent: bfloat16 [131072, 128], P(('row', 'col')), may hold values from -6 to 6
- block_count: int32 [8, 32], P('row', 'col'), may hold values from 64 to 512
- block_rows: int32 [8, 32, 512], P('row', 'col'), may hold values from 0 to 127
- block_cols: int32 [8, 32, 512], P('row', 'col'), may hold values from 0 to 31
- edge_offsets: int32 [8, 32, 512, 128], P('row', 'col'), may hold values from 0 to 16383, as said below
- edge_weight: bfloat16 [8, 32, 512, 128], P('row', 'col'), may hold values from 0.0099487305 to 0.099609375
Outputs:
- output: bfloat16 [131072, 128], P(('row', 'col'))
- grad_features: bfloat16 [131072, 128], P(('row', 'col'))
- grad_weight: float32 [128, 128], replicated
- grad_bias: float32 [128], replicated
Inputs may be any that keep to these rules, and one draw needn't show every extreme that they name: `edge_offsets`: the offsets within one slot are distinct.
All inputs are finite; a program needn't handle non-finite values.
Results may differ from a plain program's by a relative error of at most 0.013.
The roundings to bfloat16 on the way count: a program that leaves them out, or rounds other values in their place, can miss the bound.
Values may be sent and summed in bfloat16 or wider, within the bound.
A program may use at most 128 MiB of HBM per device.

v0:
```python
import jax
import jax.numpy as jnp
from jax import lax
from jax.sharding import PartitionSpec as P


def shards(
    features,
    weight,
    bias,
    cotangent,
    block_count,
    block_rows,
    block_cols,
    edge_offsets,
    edge_weight,
):
    node_dev, width = features.shape
    n_row = lax.axis_size("row")
    n_col = lax.axis_size("col")
    slots = block_rows.shape[2]
    batch = min(64, slots)
    count = block_count[0, 0]
    turns = (count + batch - 1) // batch
    brow = block_rows[0, 0]
    bcol = block_cols[0, 0]
    offsets = edge_offsets[0, 0]
    weights = edge_weight[0, 0]
    lanes = jnp.arange(batch, dtype=jnp.int32)
    within = jnp.arange(128, dtype=jnp.int32)
    row_blocks = node_dev * n_col // 128
    col_blocks = node_dev * n_row // 128
    row_ids = jnp.arange(row_blocks, dtype=jnp.int32)
    col_ids = jnp.arange(col_blocks, dtype=jnp.int32)
    projected = jnp.dot(features, weight, preferred_element_type=jnp.float32).astype(jnp.bfloat16)
    panel = lax.all_gather(projected, "row", axis=0, tiled=True).reshape(-1, 128, width)

    def forward_step(i, carry):
        stored, totals = carry
        start = i * batch
        offs = lax.dynamic_slice_in_dim(offsets, start, batch, 0)
        vals = lax.dynamic_slice_in_dim(weights, start, batch, 0).astype(jnp.float32)
        vals = jnp.where((start + lanes < count)[:, None], vals, 0.0)
        left = jnp.where((offs // 128)[:, :, None] == within, vals[:, :, None], 0.0).astype(
            jnp.bfloat16
        )
        right = ((offs % 128)[:, :, None] == within).astype(jnp.bfloat16)
        dense = jnp.einsum("bei,bej->bij", left, right, preferred_element_type=jnp.float32).astype(
            jnp.bfloat16
        )
        stored = lax.dynamic_update_slice_in_dim(stored, dense, start, 0)
        rows_here = lax.dynamic_slice_in_dim(brow, start, batch, 0)
        cols_here = lax.dynamic_slice_in_dim(bcol, start, batch, 0)
        product = jnp.einsum(
            "bij,bjf->bif", dense, panel[cols_here], preferred_element_type=jnp.float32
        )
        select = (rows_here[:, None] == row_ids).astype(jnp.float32)
        added = jnp.einsum(
            "br,bif->rif",
            select,
            product,
            precision=lax.Precision.HIGHEST,
            preferred_element_type=jnp.float32,
        )
        return (stored, totals + added)

    stored0 = jnp.zeros((slots, 128, 128), jnp.bfloat16)
    totals0 = jnp.zeros((row_blocks, 128, width), jnp.float32)
    stored, totals = lax.fori_loop(0, turns, forward_step, (stored0, totals0))
    totals = totals.reshape(-1, width)
    own = lax.psum_scatter(totals, "col", scatter_dimension=0, tiled=True)
    pre = own + bias
    output = jnp.maximum(pre, 0.0).astype(jnp.bfloat16)
    grad_own = jnp.where(pre > 0, cotangent.astype(jnp.float32), 0.0).astype(jnp.bfloat16)
    grad_panel = lax.all_gather(grad_own, "col", axis=0, tiled=True)
    grad_blocks = grad_panel.reshape(-1, 128, width)

    def backward_step(i, acc):
        start = i * batch
        dense = lax.dynamic_slice_in_dim(stored, start, batch, 0)
        rows_here = lax.dynamic_slice_in_dim(brow, start, batch, 0)
        cols_here = lax.dynamic_slice_in_dim(bcol, start, batch, 0)
        product = jnp.einsum(
            "bij,bif->bjf", dense, grad_blocks[rows_here], preferred_element_type=jnp.float32
        )
        select = (cols_here[:, None] == col_ids).astype(jnp.float32)
        added = jnp.einsum(
            "bc,bjf->cjf",
            select,
            product,
            precision=lax.Precision.HIGHEST,
            preferred_element_type=jnp.float32,
        )
        return acc + added

    acc0 = jnp.zeros((col_blocks, 128, width), jnp.float32)
    acc = lax.fori_loop(0, turns, backward_step, acc0)
    grad_proj = lax.psum_scatter(
        acc.reshape(-1, width), "row", scatter_dimension=0, tiled=True
    ).astype(jnp.bfloat16)
    grad_features = lax.dot_general(
        grad_proj, weight, (((1,), (1,)), ((), ())), preferred_element_type=jnp.float32
    ).astype(jnp.bfloat16)
    local_weight = lax.dot_general(
        features, grad_proj, (((0,), (0,)), ((), ())), preferred_element_type=jnp.float32
    )
    local_bias = jnp.sum(grad_own.astype(jnp.float32), axis=0)
    total_weight, total_bias = lax.psum((local_weight, local_bias), ("row", "col"))
    scale = (node_dev * n_row * n_col) ** (-0.5)
    return (output, grad_features, total_weight * scale, total_bias * scale)


def solution(mesh):
    return jax.shard_map(
        shards,
        mesh=mesh,
        in_specs=(
            P(("row", "col"), None),
            P(),
            P(),
            P(("row", "col"), None),
            P("row", "col"),
            P("row", "col", None),
            P("row", "col", None),
            P("row", "col", None, None),
            P("row", "col", None, None),
        ),
        out_specs=(P(("row", "col"), None), P(("row", "col"), None), P(), P()),
        check_vma=False,
    )
```

profile of v0, /device:TPU:1, one launch (start us, length us, event | category | flops | bytes accessed | tf_op | source)
XLA Modules:
  0.0 1005.6 jit_solution(10887614581579675863)
XLA Ops:
  8.1 1.6 convolution_convert_fusion.1
  10.4 34.3 %all-gather.3.cloned.1.call-done = bf16[4096,128]{1,0:T(8,128)(2,1)} async-done(((bf16[512,128]{1,0:T(8,128)(2,1)}), bf16[4096,128]{1,0:T(8,128)(2,1)}) %all-gather.3.cloned.1.call-update) | async-done | bytes 1048592 | tf_op jit(solution)/shard_map/all_gather | solution.py:36
  44.7 6.3 broadcast_in_dim.84
  51.0 4.3 broadcast_in_dim.85
  55.3 173.9 %while.29 = (s32[]{:T(128)}, bf16[512,128,128]{2,1,0:T(8,128)(2,1)}, f32[128,128,128]{2,0,1:T(8,128)}, s32[]{:T(128)}, s32[512,128]{1,0:T(8,128)}, /*index=5*/s3...) while((s32[]{:T(128)}, ...), condition=%wide.region_1.2_spmd.clone.clone, body=%wide.region_0.1_spmd.clone.clone.sunk | while | flops 2154005760 | bytes 38017104 | solution.py:69
  58.3 3.6 constant_dynamic-update-slice_fusion.2
  62.9 2.3 fusion.69
  65.3 11.7 %fusion.70 = f32[128,128,128]{2,0,1:T(8,128)} fusion(f32[128,128,128]{2,0,1:T(8,128)} %get-tuple-element.493, f32[64,128,128]{2,1,0:T(8,128)S(1)} %fusion.69, s32[64]{0:T(128)S(1)} %dynamic_slice.84), kind=kOutput, calls=%fused_computation.22.clone.1 | convolution fusion | flops 1612718080 | bytes 20971776 | tf_op jit(solution)/shard_map/while/body/br,bif->rif/dot_general | solution.py:58
  80.0 3.7 constant_dynamic-update-slice_fusion.2
  84.7 2.3 fusion.69
  87.1 11.7 %fusion.70 = f32[128,128,128]{2,0,1:T(8,128)} fusion(f32[128,128,128]{2,0,1:T(8,128)} %get-tuple-element.493, f32[64,128,128]{2,1,0:T(8,128)S(1)} %fusion.69, s32[64]{0:T(128)S(1)} %dynamic_slice.84), kind=kOutput, calls=%fused_computation.22.clone.1 | convolution fusion | flops 1612718080 | bytes 20971776 | tf_op jit(solution)/shard_map/while/body/br,bif->rif/dot_general | solution.py:58
  101.8 3.7 constant_dynamic-update-slice_fusion.2
  106.5 2.3 fusion.69
  108.9 11.7 %fusion.70 = f32[128,128,128]{2,0,1:T(8,128)} fusion(f32[128,128,128]{2,0,1:T(8,128)} %get-tuple-element.493, f32[64,128,128]{2,1,0:T(8,128)S(1)} %fusion.69, s32[64]{0:T(128)S(1)} %dynamic_slice.84), kind=kOutput, calls=%fused_computation.22.clone.1 | convolution fusion | flops 1612718080 | bytes 20971776 | tf_op jit(solution)/shard_map/while/body/br,bif->rif/dot_general | solution.py:58
  123.6 3.6 constant_dynamic-update-slice_fusion.2
  128.2 2.3 fusion.69
  130.6 11.7 %fusion.70 = f32[128,128,128]{2,0,1:T(8,128)} fusion(f32[128,128,128]{2,0,1:T(8,128)} %get-tuple-element.493, f32[64,128,128]{2,1,0:T(8,128)S(1)} %fusion.69, s32[64]{0:T(128)S(1)} %dynamic_slice.84), kind=kOutput, calls=%fused_computation.22.clone.1 | convolution fusion | flops 1612718080 | bytes 20971776 | tf_op jit(solution)/shard_map/while/body/br,bif->rif/dot_general | solution.py:58
  145.3 3.7 constant_dynamic-update-slice_fusion.2
  150.1 2.3 fusion.69
  152.4 11.7 %fusion.70 = f32[128,128,128]{2,0,1:T(8,128)} fusion(f32[128,128,128]{2,0,1:T(8,128)} %get-tuple-element.493, f32[64,128,128]{2,1,0:T(8,128)S(1)} %fusion.69, s32[64]{0:T(128)S(1)} %dynamic_slice.84), kind=kOutput, calls=%fused_computation.22.clone.1 | convolution fusion | flops 1612718080 | bytes 20971776 | tf_op jit(solution)/shard_map/while/body/br,bif->rif/dot_general | solution.py:58
  167.1 3.6 constant_dynamic-update-slice_fusion.2
  171.7 2.3 fusion.69
  174.1 11.7 %fusion.70 = f32[128,128,128]{2,0,1:T(8,128)} fusion(f32[128,128,128]{2,0,1:T(8,128)} %get-tuple-element.493, f32[64,128,128]{2,1,0:T(8,128)S(1)} %fusion.69, s32[64]{0:T(128)S(1)} %dynamic_slice.84), kind=kOutput, calls=%fused_computation.22.clone.1 | convolution fusion | flops 1612718080 | bytes 20971776 | tf_op jit(solution)/shard_map/while/body/br,bif->rif/dot_general | solution.py:58
  188.8 3.5 constant_dynamic-update-slice_fusion.2
  193.4 2.3 fusion.69
  195.8 11.7 %fusion.70 = f32[128,128,128]{2,0,1:T(8,128)} fusion(f32[128,128,128]{2,0,1:T(8,128)} %get-tuple-element.493, f32[64,128,128]{2,1,0:T(8,128)S(1)} %fusion.69, s32[64]{0:T(128)S(1)} %dynamic_slice.84), kind=kOutput, calls=%fused_computation.22.clone.1 | convolution fusion | flops 1612718080 | bytes 20971776 | tf_op jit(solution)/shard_map/while/body/br,bif->rif/dot_general | solution.py:58
  210.5 3.6 constant_dynamic-update-slice_fusion.2
  215.1 2.3 fusion.69
  217.5 11.7 %fusion.70 = f32[128,128,128]{2,0,1:T(8,128)} fusion(f32[128,128,128]{2,0,1:T(8,128)} %get-tuple-element.493, f32[64,128,128]{2,1,0:T(8,128)S(1)} %fusion.69, s32[64]{0:T(128)S(1)} %dynamic_slice.84), kind=kOutput, calls=%fused_computation.22.clone.1 | convolution fusion | flops 1612718080 | bytes 20971776 | tf_op jit(solution)/shard_map/while/body/br,bif->rif/dot_general | solution.py:58
  229.2 11.5 %copy.17 = f32[128,128,128]{2,1,0:T(8,128)} copy(f32[128,128,128]{2,0,1:T(8,128)} %get-tuple-element.240) | data formatting | bytes 16777216 | tf_op jit(solution)/shard_map/while | solution.py:69
  240.7 155.5 %reduce-scatter.3.cloned.1.call-done = f32[512,128]{1,0:T(8,128)} async-done(((f32[16384,128]{1,0:T(8,128)}), f32[512,128]{1,0:T(8,128)}) %reduce-scatter.3.cloned.1.call-update) | async-done | bytes 262160 | tf_op jit(solution)/shard_map/reduce_scatter | solution.py:71
  396.3 1.7 convert_reduce_fusion
  398.1 160.6 %all-gather.5.cloned.1.call-done = bf16[16384,128]{1,0:T(8,128)(2,1)} async-done(((bf16[512,128]{1,0:T(8,128)(2,1)}), bf16[16384,128]{1,0:T(8,128)(2,1)}) %all-gather.5.cloned.1.call-update) | async-done | bytes 4194320 | tf_op jit(solution)/shard_map/all_gather | solution.py:75
  558.7 1.6 broadcast_in_dim.86
  560.3 101.9 %while.28 = (s32[]{:T(128)}, f32[32,128,128]{2,0,1:T(8,128)}, s32[]{:T(128)}, s32[512]{0:T(512)S(1)}, bf16[512,128,128]{2,1,0:T(8,128)(2,1)}, /*index=5*/s32[512...) while((s32[]{:T(128)}, f32[32,128,128]{2,0,1:T(8,128)}, ...), condition=%wide.region_4.5_spmd.clone, body=%wide.region_3.4_spmd.clone.sunk | while | flops 671616192 | bytes 20977576 | solution.py:97
  560.4 3.1 gather_fusion
  563.5 2.5 fusion.62
  566.1 7.0 fusion.63
  573.1 3.1 gather_fusion
  576.3 2.5 fusion.62
  578.8 7.0 fusion.63
  585.9 3.1 gather_fusion
  589.0 2.5 fusion.62
  591.5 7.0 fusion.63
  598.6 3.1 gather_fusion
  601.7 2.5 fusion.62
  604.3 7.0 fusion.63
  611.3 3.1 gather_fusion
  614.5 2.5 fusion.62
  617.0 7.0 fusion.63
  624.1 3.1 gather_fusion
  627.2 2.5 fusion.62
  629.8 7.0 fusion.63
  636.8 3.1 gather_fusion
  640.0 2.5 fusion.62
  642.5 7.0 fusion.63
  649.6 3.1 gather_fusion
  652.7 2.5 fusion.62
  655.2 7.0 fusion.63
  662.2 4.1 copy.18
  666.4 93.1 %psum.15 = f32[128]{0:T(128)S(1)} all-reduce(f32[128]{0:T(128)S(1)} %get-tuple-element.358), channel_id=1, replica_groups=mesh['row'=8,'col'=32] {'row','col'}, use_global_device_ids=true, to_apply=%region_8.9 | all-reduce | flops 128 | bytes 1024 | tf_op jit(solution)/shard_map/psum | solution.py:108
  760.1 1.8 convolution_bitcast_fusion
  761.9 1.8 convolution_convert_fusion
  763.7 233.7 %all-reduce.2.cloned.1.call-done = f32[128,128]{0,1:T(8,128)} async-done(((f32[128,128]{0,1:T(8,128)}), f32[128,128]{0,1:T(8,128)}) %all-reduce.2.cloned.1.call-update) | async-done | bytes 65552 | tf_op jit(solution)/shard_map/psum | solution.py:108
  (116 shorter events, 37.6 us)
Async XLA Ops:
  7.2 0.9 copy-start
  7.2 37.5 %all-gather.3.cloned.1.call-start = ((), (), s32[]{:S(2)}) async-start(), calls=%async_computation.2 | async-start | bytes 1179648 | tf_op jit(solution)/shard_map/all_gather | solution.py:36
  9.7 386.6 %reduce-scatter.3.cloned.1.call-start = ((), (), s32[]{:S(2)}) async-start(), calls=%async_computation.3 | async-start | bytes 8650752 | tf_op jit(solution)/shard_map/reduce_scatter | solution.py:71
  51.0 4.3 copy-start.1
  51.0 4.3 copy-start.5
  51.0 4.3 copy-start.6
  240.7 155.6 %copy-start.2 = (bf16[512,128]{1,0:T(8,128)(2,1)S(1)}, bf16[512,128]{1,0:T(8,128)(2,1)}, u32[]{:S(2)}) copy-start(bf16[512,128]{1,0:T(8,128)(2,1)} %param.16) | copy-start | bytes 393220
  240.7 155.6 %copy-start.4 = (f32[128]{0:T(128)S(1)}, f32[128]{0:T(128)}, u32[]{:S(2)}) copy-start(f32[128]{0:T(128)} %param.15) | copy-start | bytes 1540
  240.7 318.0 %all-gather.5.cloned.1.call-start = ((), (), s32[]{:S(2)}) async-start(), calls=%async_computation.4 | async-start | bytes 4325376 | tf_op jit(solution)/shard_map/all_gather | solution.py:75
  398.0 362.1 %reduce-scatter.5.cloned.1.call-start = ((), (), s32[]{:S(2)}) async-start(), calls=%async_computation.5 | async-start | bytes 2359296 | tf_op jit(solution)/shard_map/reduce_scatter | solution.py:98
  662.2 99.7 %copy-start.3 = (bf16[128,128]{1,0:T(8,128)(2,1)S(1)}, bf16[128,128]{1,0:T(8,128)(2,1)}, u32[]{:S(2)}) copy-start(bf16[128,128]{1,0:T(8,128)(2,1)} %param.14) | copy-start | bytes 98308
  666.4 331.1 %all-reduce.2.cloned.1.call-start = ((), (), s32[]{:S(2)}) async-start(), calls=%async_computation.6 | async-start | bytes 131072 | tf_op jit(solution)/shard_map/psum | solution.py:108
Sparse Core Ops, SparseCore 0:
  10.4 34.2 all-gather.2
  240.8 155.4 reduce-scatter.2
  398.6 160.0 all-gather.4
  666.5 58.0 reduce-scatter.4
  762.0 235.3 all-reduce.1
where the time goes:
time: 1010 us
  waiting for transfers between devices  584 us (58%)
  matrix products  221 us (22%)
  blocking collectives  93.1 us (9%)
  local copies, waits for them, and re-layouts  63.3 us (6%)
  other arithmetic  28.6 us (3%)
  between operations  14.5 us (1%)
    psum x1, waiting for transfers between devices, shards(): lax.psum((local_weight, local_bias), ('row', 'col'))  234 us
    all_gather x1, waiting for transfers between devices, shards(): grad_panel = lax.all_gather(grad_own, 'col', axis=0, tiled=True)  161 us
    reduce_scatter x1, waiting for transfers between devices, shards(): own = lax.psum_scatter(totals, 'col', scatter_dimension=0, tiled=True)  156 us
    dot_general x8, matrix products, forward_step(): jnp.einsum('br,bif->rif', select, product, precision=lax.Precision.HIGHES...  93.5 us
    psum x1, blocking collectives, shards(): lax.psum((local_weight, local_bias), ('row', 'col'))  93.1 us
    dot_general x8, matrix products, backward_step(): jnp.einsum('bc,bjf->cjf', select, product, precision=lax.Precision.HIGHES...  55.8 us
    all_gather x1, waiting for transfers between devices, shards(): lax.all_gather(projected, 'row', axis=0, tiled=True).reshape(-1, 128, width)  34.3 us
    dot_general x8, matrix products, forward_step(): jnp.einsum('bei,bej->bij', left, right, preferred_element_type=jnp.float32)  28.9 us
  transfers between devices with their start and end apart: 5, of which 4 were waited for; matrix products, arithmetic and copies ran while one was open for 0% of the time, Pallas kernels for 0%

commit v1 on v0

--- a/solution.py
+++ b/solution.py
@@ -105,7 +105,7 @@
         features, grad_proj, (((0,), (0,)), ((), ())), preferred_element_type=jnp.float32
     )
     local_bias = jnp.sum(grad_own.astype(jnp.float32), axis=0)
-    total_weight, total_bias = lax.psum((local_weight, local_bias), ("row", "col"))
+    total_weight, total_bias = lax.psum(lax.psum((local_weight, local_bias), "col"), "row")
     scale = (node_dev * n_row * n_col) ** (-0.5)
     return (output, grad_features, total_weight * scale, total_bias * scale)
 

time: 1010 us -> 1140 us (1.13)
  waiting for transfers between devices: 584 us -> 692 us
  blocking collectives: 93.1 us -> 112 us
    psum x1 -> x2, waiting for transfers between devices: 234 us -> 341 us  [the longest x1 258 us: shards(): lax.psum((local_weight, local_bias), 'col')]
    psum x1 -> x2, blocking collectives: 93.1 us -> 112 us  [the longest x1 67.9 us: shards(): lax.psum((local_weight, local_bias), 'col')]
  transfers between devices with their start and end apart: 5 -> 6, of which waited for: 4 -> 5; matrix products, arithmetic and copies ran while one was open for 0% -> 0% of each run, Pallas kernels for 0% -> 0%
where the time goes in v1:
time: 1140 us; the launch traced here: 1130 us
  waiting for transfers between devices  692 us (61%)
  matrix products  221 us (19%)
  blocking collectives  112 us (10%)
  local copies, waits for them, and re-layouts  63.3 us (6%)
  other arithmetic  28.6 us (3%)
  between operations  14.8 us (1%)
    psum x1, waiting for transfers between devices, shards(): lax.psum((local_weight, local_bias), 'col')  258 us
    all_gather x1, waiting for transfers between devices, shards(): grad_panel = lax.all_gather(grad_own, 'col', axis=0, tiled=True)  159 us
    reduce_scatter x1, waiting for transfers between devices, shards(): own = lax.psum_scatter(totals, 'col', scatter_dimension=0, tiled=True)  157 us
    dot_general x8, matrix products, forward_step(): jnp.einsum('br,bif->rif', select, product, precision=lax.Precision.HIGHES...  93.5 us
    psum x1, waiting for transfers between devices, shards(): lax.psum(lax.psum((local_weight, local_bias), 'col'), 'row')  83.1 us
    psum x1, blocking collectives, shards(): lax.psum((local_weight, local_bias), 'col')  67.9 us
    dot_general x8, matrix products, backward_step(): jnp.einsum('bc,bjf->cjf', select, product, precision=lax.Precision.HIGHES...  55.7 us
    psum x1, blocking collectives, shards(): lax.psum(lax.psum((local_weight, local_bias), 'col'), 'row')  44.1 us
  transfers between devices with their start and end apart: 6, of which 5 were waited for; matrix products, arithmetic and copies ran while one was open for 0% of the time, Pallas kernels for 0%

profile of v1, /device:TPU:1, one launch (start us, length us, event | category | flops | bytes accessed | tf_op | source)
XLA Modules:
  0.0 1132.1 jit_solution(6818757277769979306)
XLA Ops:
  10.4 34.3 %all-gather.3.cloned.1.call-done = bf16[4096,128]{1,0:T(8,128)(2,1)} async-done(((bf16[512,128]{1,0:T(8,128)(2,1)}), bf16[4096,128]{1,0:T(8,128)(2,1)}) %all-gather.3.cloned.1.call-update) | async-done | bytes 1048592 | tf_op jit(solution)/shard_map/all_gather | solution.py:36
  44.7 6.3 broadcast_in_dim.84
  51.0 4.3 broadcast_in_dim.85
  55.3 174.0 %while.29 = (s32[]{:T(128)}, bf16[512,128,128]{2,1,0:T(8,128)(2,1)}, f32[128,128,128]{2,0,1:T(8,128)}, s32[]{:T(128)}, s32[512,128]{1,0:T(8,128)}, /*index=5*/s3...) while((s32[]{:T(128)}, ...), condition=%wide.region_1.2_spmd.clone.clone, body=%wide.region_0.1_spmd.clone.clone.sunk | while | flops 2154005760 | bytes 38017104 | solution.py:69
  58.4 3.6 constant_dynamic-update-slice_fusion.2
  63.0 2.3 fusion.69
  65.3 11.7 %fusion.70 = f32[128,128,128]{2,0,1:T(8,128)} fusion(f32[128,128,128]{2,0,1:T(8,128)} %get-tuple-element.493, f32[64,128,128]{2,1,0:T(8,128)S(1)} %fusion.69, s32[64]{0:T(128)S(1)} %dynamic_slice.84), kind=kOutput, calls=%fused_computation.22.clone.1 | convolution fusion | flops 1612718080 | bytes 20971776 | tf_op jit(solution)/shard_map/while/body/br,bif->rif/dot_general | solution.py:58
  80.1 3.6 constant_dynamic-update-slice_fusion.2
  84.8 2.3 fusion.69
  87.1 11.7 %fusion.70 = f32[128,128,128]{2,0,1:T(8,128)} fusion(f32[128,128,128]{2,0,1:T(8,128)} %get-tuple-element.493, f32[64,128,128]{2,1,0:T(8,128)S(1)} %fusion.69, s32[64]{0:T(128)S(1)} %dynamic_slice.84), kind=kOutput, calls=%fused_computation.22.clone.1 | convolution fusion | flops 1612718080 | bytes 20971776 | tf_op jit(solution)/shard_map/while/body/br,bif->rif/dot_general | solution.py:58
  101.8 3.7 constant_dynamic-update-slice_fusion.2
  106.5 2.3 fusion.69
  108.9 11.7 %fusion.70 = f32[128,128,128]{2,0,1:T(8,128)} fusion(f32[128,128,128]{2,0,1:T(8,128)} %get-tuple-element.493, f32[64,128,128]{2,1,0:T(8,128)S(1)} %fusion.69, s32[64]{0:T(128)S(1)} %dynamic_slice.84), kind=kOutput, calls=%fused_computation.22.clone.1 | convolution fusion | flops 1612718080 | bytes 20971776 | tf_op jit(solution)/shard_map/while/body/br,bif->rif/dot_general | solution.py:58
  123.6 3.6 constant_dynamic-update-slice_fusion.2
  128.3 2.3 fusion.69
  130.6 11.7 %fusion.70 = f32[128,128,128]{2,0,1:T(8,128)} fusion(f32[128,128,128]{2,0,1:T(8,128)} %get-tuple-element.493, f32[64,128,128]{2,1,0:T(8,128)S(1)} %fusion.69, s32[64]{0:T(128)S(1)} %dynamic_slice.84), kind=kOutput, calls=%fused_computation.22.clone.1 | convolution fusion | flops 1612718080 | bytes 20971776 | tf_op jit(solution)/shard_map/while/body/br,bif->rif/dot_general | solution.py:58
  145.3 3.7 constant_dynamic-update-slice_fusion.2
  150.1 2.3 fusion.69
  152.5 11.7 %fusion.70 = f32[128,128,128]{2,0,1:T(8,128)} fusion(f32[128,128,128]{2,0,1:T(8,128)} %get-tuple-element.493, f32[64,128,128]{2,1,0:T(8,128)S(1)} %fusion.69, s32[64]{0:T(128)S(1)} %dynamic_slice.84), kind=kOutput, calls=%fused_computation.22.clone.1 | convolution fusion | flops 1612718080 | bytes 20971776 | tf_op jit(solution)/shard_map/while/body/br,bif->rif/dot_general | solution.py:58
  167.2 3.6 constant_dynamic-update-slice_fusion.2
  171.8 2.3 fusion.69
  174.2 11.7 %fusion.70 = f32[128,128,128]{2,0,1:T(8,128)} fusion(f32[128,128,128]{2,0,1:T(8,128)} %get-tuple-element.493, f32[64,128,128]{2,1,0:T(8,128)S(1)} %fusion.69, s32[64]{0:T(128)S(1)} %dynamic_slice.84), kind=kOutput, calls=%fused_computation.22.clone.1 | convolution fusion | flops 1612718080 | bytes 20971776 | tf_op jit(solution)/shard_map/while/body/br,bif->rif/dot_general | solution.py:58
  188.9 3.6 constant_dynamic-update-slice_fusion.2
  193.5 2.3 fusion.69
  195.9 11.7 %fusion.70 = f32[128,128,128]{2,0,1:T(8,128)} fusion(f32[128,128,128]{2,0,1:T(8,128)} %get-tuple-element.493, f32[64,128,128]{2,1,0:T(8,128)S(1)} %fusion.69, s32[64]{0:T(128)S(1)} %dynamic_slice.84), kind=kOutput, calls=%fused_computation.22.clone.1 | convolution fusion | flops 1612718080 | bytes 20971776 | tf_op jit(solution)/shard_map/while/body/br,bif->rif/dot_general | solution.py:58
  210.6 3.6 constant_dynamic-update-slice_fusion.2
  215.2 2.3 fusion.69
  217.6 11.7 %fusion.70 = f32[128,128,128]{2,0,1:T(8,128)} fusion(f32[128,128,128]{2,0,1:T(8,128)} %get-tuple-element.493, f32[64,128,128]{2,1,0:T(8,128)S(1)} %fusion.69, s32[64]{0:T(128)S(1)} %dynamic_slice.84), kind=kOutput, calls=%fused_computation.22.clone.1 | convolution fusion | flops 1612718080 | bytes 20971776 | tf_op jit(solution)/shard_map/while/body/br,bif->rif/dot_general | solution.py:58
  229.3 11.5 %copy.17 = f32[128,128,128]{2,1,0:T(8,128)} copy(f32[128,128,128]{2,0,1:T(8,128)} %get-tuple-element.240) | data formatting | bytes 16777216 | tf_op jit(solution)/shard_map/while | solution.py:69
  240.8 156.7 %reduce-scatter.3.cloned.1.call-done = f32[512,128]{1,0:T(8,128)} async-done(((f32[16384,128]{1,0:T(8,128)}), f32[512,128]{1,0:T(8,128)}) %reduce-scatter.3.cloned.1.call-update) | async-done | bytes 262160 | tf_op jit(solution)/shard_map/reduce_scatter | solution.py:71
  397.6 1.7 convert_reduce_fusion
  399.4 159.1 %all-gather.5.cloned.1.call-done = bf16[16384,128]{1,0:T(8,128)(2,1)} async-done(((bf16[512,128]{1,0:T(8,128)(2,1)}), bf16[16384,128]{1,0:T(8,128)(2,1)}) %all-gather.5.cloned.1.call-update) | async-done | bytes 4194320 | tf_op jit(solution)/shard_map/all_gather | solution.py:75
  560.1 101.9 %while.28 = (s32[]{:T(128)}, f32[32,128,128]{2,0,1:T(8,128)}, s32[]{:T(128)}, s32[512]{0:T(512)S(1)}, bf16[512,128,128]{2,1,0:T(8,128)(2,1)}, /*index=5*/s32[512...) while((s32[]{:T(128)}, f32[32,128,128]{2,0,1:T(8,128)}, ...), condition=%wide.region_4.5_spmd.clone, body=%wide.region_3.4_spmd.clone.sunk | while | flops 671616192 | bytes 20977576 | solution.py:97
  560.1 3.1 gather_fusion
  563.3 2.5 fusion.62
  565.8 7.0 fusion.63
  572.9 3.1 gather_fusion
  576.0 2.5 fusion.62
  578.6 7.0 fusion.63
  585.6 3.1 gather_fusion
  588.8 2.5 fusion.62
  591.3 7.0 fusion.63
  598.4 3.1 gather_fusion
  601.5 2.5 fusion.62
  604.0 7.0 fusion.63
  611.1 3.1 gather_fusion
  614.2 2.5 fusion.62
  616.8 7.0 fusion.63
  623.8 3.1 gather_fusion
  627.0 2.5 fusion.62
  629.5 7.0 fusion.63
  636.6 3.1 gather_fusion
  639.7 2.5 fusion.62
  642.3 7.0 fusion.63
  649.3 3.1 gather_fusion
  652.5 2.5 fusion.62
  655.0 7.0 fusion.63
  662.0 4.2 copy.18
  666.2 67.9 %psum.30 = f32[128]{0:T(128)S(1)} all-reduce(f32[128]{0:T(128)S(1)} %get-tuple-element.358), channel_id=1, replica_groups=mesh['row'=8,'col'=32] {'col'}, use_global_device_ids=true, to_apply=%region_9.10 | all-reduce | flops 128 | bytes 1024 | tf_op jit(solution)/shard_map/psum | solution.py:108
  734.1 44.1 %psum.31 = f32[128]{0:T(128)S(1)} all-reduce(f32[128]{0:T(128)S(1)} %psum.30), channel_id=1, replica_groups=mesh['row'=8,'col'=32] {'row'}, use_global_device_ids=true, to_apply=%region_10.11 | all-reduce | flops 128 | bytes 1024 | tf_op jit(solution)/shard_map/psum | solution.py:108
  778.2 1.8 convolution_bitcast_fusion
  780.6 258.2 %all-reduce.3.cloned.1.call-done = f32[128,128]{0,1:T(8,128)} async-done(((f32[128,128]{0,1:T(8,128)}), f32[128,128]{0,1:T(8,128)}) %all-reduce.3.cloned.1.call-update) | async-done | bytes 65552 | tf_op jit(solution)/shard_map/psum | solution.py:108
  1038.8 1.8 convolution_convert_fusion
  1040.6 83.1 %all-reduce.5.cloned.1.call-done = f32[128,128]{0,1:T(8,128)} async-done(((f32[128,128]{0,1:T(8,128)}), f32[128,128]{0,1:T(8,128)}) %all-reduce.5.cloned.1.call-update) | async-done | bytes 65552 | tf_op jit(solution)/shard_map/psum | solution.py:108
  (120 shorter events, 40.8 us)
Async XLA Ops:
  7.2 0.9 copy-start
  7.2 37.5 %all-gather.3.cloned.1.call-start = ((), (), s32[]{:S(2)}) async-start(), calls=%async_computation.2 | async-start | bytes 1179648 | tf_op jit(solution)/shard_map/all_gather | solution.py:36
  9.7 387.9 %reduce-scatter.3.cloned.1.call-start = ((), (), s32[]{:S(2)}) async-start(), calls=%async_computation.3 | async-start | bytes 8650752 | tf_op jit(solution)/shard_map/reduce_scatter | solution.py:71
  51.0 4.3 copy-start.1
  51.0 4.3 copy-start.5
  51.0 4.3 copy-start.6
  240.7 156.8 %copy-start.2 = (bf16[512,128]{1,0:T(8,128)(2,1)S(1)}, bf16[512,128]{1,0:T(8,128)(2,1)}, u32[]{:S(2)}) copy-start(bf16[512,128]{1,0:T(8,128)(2,1)} %param.16) | copy-start | bytes 393220
  240.7 156.8 %copy-start.4 = (f32[128]{0:T(128)S(1)}, f32[128]{0:T(128)}, u32[]{:S(2)}) copy-start(f32[128]{0:T(128)} %param.15) | copy-start | bytes 1540
  240.8 317.7 %all-gather.5.cloned.1.call-start = ((), (), s32[]{:S(2)}) async-start(), calls=%async_computation.4 | async-start | bytes 4325376 | tf_op jit(solution)/shard_map/all_gather | solution.py:75
  399.3 378.9 %reduce-scatter.5.cloned.1.call-start = ((), (), s32[]{:S(2)}) async-start(), calls=%async_computation.5 | async-start | bytes 2359296 | tf_op jit(solution)/shard_map/reduce_scatter | solution.py:98
  662.0 376.8 %copy-start.3 = (bf16[128,128]{1,0:T(8,128)(2,1)S(1)}, bf16[128,128]{1,0:T(8,128)(2,1)}, u32[]{:S(2)}) copy-start(bf16[128,128]{1,0:T(8,128)(2,1)} %param.14) | copy-start | bytes 98308
  666.1 372.6 %all-reduce.3.cloned.1.call-start = ((), (), s32[]{:S(2)}) async-start(), calls=%async_computation.6 | async-start | bytes 131072 | tf_op jit(solution)/shard_map/psum | solution.py:108
  780.0 343.7 %all-reduce.5.cloned.1.call-start = ((), (), s32[]{:S(2)}) async-start(), calls=%async_computation.7 | async-start | bytes 131072 | tf_op jit(solution)/shard_map/psum | solution.py:108
Sparse Core Ops, SparseCore 0:
  10.4 34.2 all-gather.2
  240.9 156.6 reduce-scatter.2
  399.9 158.4 all-gather.4
  666.3 57.4 reduce-scatter.4
  780.1 258.5 all-reduce.2
  1041.4 82.2 all-reduce.4
